TPU v7x, 256 devices: a whole 4x4x8 slice. The times are simulated.
256 devices in a mesh: seq: 32 (over y, z), head: 8 (over x, core).
Axes of the slice: x: 4, y: 4, z: 8, core: 2. Of those that a mesh axis runs over, the one named last changes fastest.
Arguments:
- new_query: bfloat16 [96, 4, 4096], P(None, None, 'head'), may hold values from -40 to 40
- fresh_key_value: bfloat16 [96, 4, 8, 128], P('seq', None, 'head'), may hold values from -24 to 24
- prompt_cache: bfloat16 [8, 32768, 8, 128], P(None, 'seq', 'head'), may hold values from -30 to 30
- decoded_tail_cache: bfloat16 [96, 1024, 8, 128], P(None, 'seq', 'head'), may hold values from -6 to 6
- sinks: float32 [64], P('head'), may hold values from 2 to 14
- prompt_group: int32 [96], replicated, may hold values from 0 to 7, as said below
- prompt_lens: int32 [8], replicated, may hold values from 1 to 32768
- tail_lens: int32 [96], replicated, may hold values from 0 to 1024
- o_weight: bfloat16 [4096, 2880], P('head'), may hold values from -0.09375 to 0.09375
- resid: bfloat16 [96, 4, 2880], P('seq'), may hold values from -1.796875 to 1.796875
- norm_gain: float32 [2880], replicated, may hold values from 0.3 to 3
- expert_ids: int32 [96, 4, 4], replicated, may hold values from 0 to 31, all different within a row; in each aligned block of 12 rows (0 to 11, 12 to 23, ..., all dimensions but the last counted through in order) at most 3 rows name the same one
- route_weights: float32 [96, 4, 4], P('seq'), may hold values from 0.05 to 0.6
- gate_up: bfloat16 [32, 2880, 2, 2880], P('seq', None, None, 'head'), may hold values from -0.3125 to 0.3125
- down_weight: bfloat16 [32, 2880, 2880], P('seq', 'head'), may hold values from -0.0390625 to 0.0390625
Outputs:
- output: bfloat16 [96, 4, 2880], P('seq')
Inputs may be any that keep to these rules, and one draw needn't show every extreme that they name: `prompt_group`: each of the 8 groups holds exactly 12 requests. `expert_ids`: a token's 4 picks are distinct; among the 12 tokens of the requests s * 3 to (s + 1) * 3 - 1 no expert is picked more than 3 times.
All inputs are finite; a program needn't handle non-finite values.
Results may differ from a plain program's by a relative error of at most 0.025.
Values may be sent and summed in bfloat16 or wider, within the bound.
A program may use at most 128 MiB of HBM per device.

v0:
```python
import math
import jax
import jax.numpy as jnp
from jax import lax
from jax.sharding import PartitionSpec as P

very_low = -1e30


def rotate(vector, position):
    half_width = vector.shape[-1] // 2
    frequency = jnp.exp(
        jnp.arange(half_width, dtype=jnp.float32) * (-2.0 * math.log(150000.0) / vector.shape[-1])
    )
    angle = position[..., None] * frequency
    cosine = jnp.cos(angle)
    sine_part = jnp.sin(angle)
    leading = vector[..., :half_width]
    trailing = vector[..., half_width:]
    return jnp.concatenate(
        [leading * cosine - trailing * sine_part, trailing * cosine + leading * sine_part], axis=-1
    )


def block_weights(scores, valid):
    masked = jnp.where(valid, scores, very_low)
    highest = jnp.max(masked, axis=-1)
    weights = jnp.where(valid, jnp.exp(masked - highest[..., None]), 0.0)
    return (highest, jnp.sum(weights, axis=-1), weights)


def joined_stats(first, second):
    highest_a, total_a, weighted_a = first
    highest_b, total_b, weighted_b = second
    highest = jnp.maximum(highest_a, highest_b)
    factor_a = jnp.exp(highest_a - highest)
    factor_b = jnp.exp(highest_b - highest)
    spread_count = weighted_a.shape[-1] // highest_a.shape[-1]
    weighted = weighted_a * jnp.repeat(factor_a, spread_count, axis=-1) + weighted_b * jnp.repeat(
        factor_b, spread_count, axis=-1
    )
    return (highest, total_a * factor_a + total_b * factor_b, weighted)


def slot_numbers(picks, experts_total):
    one_hot = (picks[..., None] == jnp.arange(experts_total, dtype=jnp.int32)).astype(jnp.int32)
    earlier = jnp.cumsum(one_hot, axis=-2) - one_hot
    return jnp.sum(earlier * one_hot, axis=-1)


def on_device(
    new_query,
    fresh_key_value,
    prompt_cache,
    decoded_tail_cache,
    sinks,
    prompt_group,
    prompt_lens,
    tail_lens,
    o_weight,
    resid,
    norm_gain,
    expert_ids,
    route_weights,
    gate_up,
    down_weight,
):
    seq_count = lax.axis_size("seq")
    seq_index = lax.axis_index("seq")
    groups_total, prompt_block, kv_local, double_width = prompt_cache.shape
    head_dim = double_width // 2
    requests, steps_total, query_width = new_query.shape
    heads_local = query_width // head_dim
    requests_per_group = heads_local // kv_local
    owned = fresh_key_value.shape[0]
    tail_block = decoded_tail_cache.shape[1]
    group_size = requests // groups_total
    model_width = resid.shape[-1]
    factor_scale = 1.0 / math.sqrt(head_dim)
    first_row = seq_index * owned
    group_hot = prompt_group[:, None] == jnp.arange(groups_total, dtype=jnp.int32)[None, :]
    prompt_start = jnp.sum(jnp.where(group_hot, prompt_lens[None, :], 0), axis=1)
    positions = (
        (prompt_start + tail_lens)[:, None] + jnp.arange(steps_total, dtype=jnp.int32)[None, :]
    ).astype(jnp.float32)
    query_matrix = new_query.reshape(requests, steps_total, heads_local, head_dim).astype(
        jnp.float32
    )
    rotated = rotate(query_matrix, positions[:, :, None]).astype(jnp.bfloat16)
    rotated = rotated.reshape(requests, steps_total, kv_local, requests_per_group, head_dim)
    ordering = jnp.argsort(prompt_group, stable=True)
    inverse = jnp.zeros_like(ordering).at[ordering].set(jnp.arange(requests, dtype=jnp.int32))
    grouped = rotated[ordering].reshape(
        groups_total, group_size, steps_total, kv_local, requests_per_group, head_dim
    )
    prompt_scores = (
        jnp.einsum(
            "grtcjd,gpcd->grtcjp",
            grouped,
            prompt_cache[..., :head_dim],
            preferred_element_type=jnp.float32,
        )
        * factor_scale
    )
    prompt_valid = (seq_index * prompt_block + jnp.arange(prompt_block, dtype=jnp.int32))[
        None, :
    ] < prompt_lens[:, None]
    prompt_high, prompt_total, prompt_weights = block_weights(
        prompt_scores, prompt_valid[:, None, None, None, None, :]
    )
    prompt_acc = jnp.einsum(
        "grtcjp,gpcd->grtcjd",
        prompt_weights.astype(jnp.bfloat16),
        prompt_cache[..., head_dim:],
        preferred_element_type=jnp.float32,
    )
    prompt_stats = (
        prompt_high.reshape(requests, steps_total, heads_local)[inverse],
        prompt_total.reshape(requests, steps_total, heads_local)[inverse],
        prompt_acc.reshape(requests, steps_total, query_width)[inverse],
    )
    tail_scores = (
        jnp.einsum(
            "rtcjd,rucd->rtcju",
            rotated,
            decoded_tail_cache[..., :head_dim],
            preferred_element_type=jnp.float32,
        )
        * factor_scale
    )
    tail_valid = (seq_index * tail_block + jnp.arange(tail_block, dtype=jnp.int32))[
        None, :
    ] < tail_lens[:, None]
    tail_high, tail_total, tail_weights = block_weights(
        tail_scores, tail_valid[:, None, None, None, :]
    )
    tail_acc = jnp.einsum(
        "rtcju,rucd->rtcjd",
        tail_weights.astype(jnp.bfloat16),
        decoded_tail_cache[..., head_dim:],
        preferred_element_type=jnp.float32,
    )
    tail_stats = (
        tail_high.reshape(requests, steps_total, heads_local),
        tail_total.reshape(requests, steps_total, heads_local),
        tail_acc.reshape(requests, steps_total, query_width),
    )
    local_stats = joined_stats(prompt_stats, tail_stats)
    own_query = lax.dynamic_slice_in_dim(rotated, first_row, owned, 0)
    own_positions = lax.dynamic_slice_in_dim(positions, first_row, owned, 0)
    fresh_keys = rotate(
        fresh_key_value[..., :head_dim].astype(jnp.float32), own_positions[:, :, None]
    ).astype(jnp.bfloat16)
    fresh_scores = (
        jnp.einsum("rtcjd,rucd->rtcju", own_query, fresh_keys, preferred_element_type=jnp.float32)
        * factor_scale
    )
    causal = jnp.arange(steps_total)[None, :] <= jnp.arange(steps_total)[:, None]
    fresh_high, fresh_total, fresh_weights = block_weights(
        fresh_scores, causal[None, :, None, None, :]
    )
    fresh_acc = jnp.einsum(
        "rtcju,rucd->rtcjd",
        fresh_weights.astype(jnp.bfloat16),
        fresh_key_value[..., head_dim:],
        preferred_element_type=jnp.float32,
    )
    fresh_stats = (
        fresh_high.reshape(owned, steps_total, heads_local),
        fresh_total.reshape(owned, steps_total, heads_local),
        fresh_acc.reshape(owned, steps_total, query_width),
    )
    by_owner = tuple(
        (member.reshape((seq_count, owned) + member.shape[1:]) for member in local_stats)
    )
    recv_high, recv_total, recv_acc = (
        lax.all_to_all(by_owner[0], "seq", split_axis=0, concat_axis=0, tiled=True),
        lax.all_to_all(by_owner[1], "seq", split_axis=0, concat_axis=0, tiled=True),
        lax.all_to_all(by_owner[2], "seq", split_axis=0, concat_axis=0, tiled=True),
    )
    owner_high = jnp.max(recv_high, axis=0)
    factors = jnp.exp(recv_high - owner_high[None])
    owner_total = jnp.sum(recv_total * factors, axis=0)
    owner_acc = jnp.sum(recv_acc * jnp.repeat(factors, head_dim, axis=-1), axis=0)
    final_stats = joined_stats((owner_high, owner_total, owner_acc), fresh_stats)
    final_high, final_total, final_acc = final_stats
    with_sink = jnp.maximum(final_high, sinks)
    kept = jnp.exp(final_high - with_sink)
    denom_total = final_total * kept + jnp.exp(sinks - with_sink)
    attended = (final_acc * jnp.repeat(kept / denom_total, head_dim, axis=-1)).astype(jnp.bfloat16)
    token_count = owned * steps_total
    partial_proj = jnp.dot(
        attended.reshape(token_count, query_width), o_weight, preferred_element_type=jnp.float32
    )
    projected = lax.psum(partial_proj, "head")
    hidden = (resid.reshape(token_count, model_width).astype(jnp.float32) + projected).astype(
        jnp.bfloat16
    )
    wide = hidden.astype(jnp.float32)
    normed = (
        wide * lax.rsqrt(jnp.mean(wide * wide, axis=-1, keepdims=True) + 1e-05) * norm_gain
    ).astype(jnp.bfloat16)
    experts_local = gate_up.shape[0]
    hidden_local = gate_up.shape[-1]
    experts_total = experts_local * seq_count
    top_count = expert_ids.shape[-1]
    capacity = token_count * top_count // experts_total + 2
    pair_count = token_count * top_count
    all_picks = expert_ids.reshape(seq_count, pair_count)
    own_picks = lax.dynamic_slice_in_dim(all_picks, seq_index, 1, 0)[0]
    own_index = own_picks * capacity + slot_numbers(own_picks, experts_total)
    pair_token = jnp.arange(pair_count, dtype=jnp.int32) // top_count
    joined_weight = gate_up.reshape(experts_local, model_width, 2 * hidden_local)
    outgoing = (
        jnp.zeros((experts_total * capacity, model_width), jnp.bfloat16)
        .at[own_index]
        .set(normed[pair_token])
    )
    outgoing = outgoing.reshape(seq_count, experts_local, capacity, model_width)
    projected_rows = jnp.einsum(
        "nekd,edf->nekf",
        lax.all_to_all(outgoing, "seq", split_axis=0, concat_axis=0, tiled=True),
        joined_weight,
        preferred_element_type=jnp.float32,
    )
    gate_part = jnp.minimum(projected_rows[..., :hidden_local], 7.0)
    up_part = jnp.clip(projected_rows[..., hidden_local:], -7.0, 7.0)
    activation = ((up_part + 1.0) * gate_part * jax.nn.sigmoid(1.702 * gate_part)).astype(
        jnp.bfloat16
    )
    returned = lax.all_to_all(
        jnp.einsum("nekf,efd->nekd", activation, down_weight, preferred_element_type=jnp.float32),
        "seq",
        split_axis=0,
        concat_axis=0,
        tiled=True,
    )
    back_rows = returned.reshape(experts_total * capacity, model_width)[own_index]
    weighted = back_rows.reshape(token_count, top_count, model_width) * route_weights.reshape(
        token_count, top_count, 1
    )
    expert_part = jnp.sum(weighted, axis=1)
    expert_total = lax.psum(expert_part, "head")
    return (wide + expert_total).astype(jnp.bfloat16).reshape(owned, steps_total, model_width)


def solution(mesh):
    return jax.shard_map(
        on_device,
        mesh=mesh,
        in_specs=(
            P(None, None, "head"),
            P("seq", None, "head", None),
            P(None, "seq", "head", None),
            P(None, "seq", "head", None),
            P("head"),
            P(),
            P(),
            P(),
            P("head", None),
            P("seq", None, None),
            P(),
            P(),
            P("seq", None, None),
            P("seq", None, None, "head"),
            P("seq", "head", None),
        ),
        out_specs=P("seq", None, None),
        check_vma=False,
    )
```

profile of v0, /device:TPU:8, one launch (start us, length us, event | category | flops | bytes accessed | tf_op | source)
XLA Modules:
  0.0 368.7 jit_solution(5805711957272378757)
XLA Ops:
  7.5 3.2 sort.17
  16.9 3.4 copy.153
  29.1 2.7 gather_fusion
  31.8 3.7 %fusion.1 = (f32[8,12,4,8]{3,2,1,0:T(4,128)S(1)}, f32[8,12,4,8,1024]{4,3,2,1,0:T(8,128)S(1)}) fusion(pred[8,1024]{1,0:T(8,128)(4,1)S(1)} %broadcast_compare_fusion.1, bf16[8,12,4,8,64]{4,3,2,1,0:T(8,128)(2,1)} %bitcast.215, bf16[8,1024,1,128]{3,1,2,0:T(8,128)(2,1)} %param.17), kind=kOutput, calls=%fused_computation.11 | convolution fusion | flops 412087296 | bytes 15093760 | tf_op jit(solution)/shard_map/grtcjd,gpcd->grtcjp/dot_general | solution.py:97
  35.6 4.0 %fusion.2 = f32[8,12,4,8]{3,2,1,0:T(4,128)S(1)} fusion(f32[8,12,4,8,1024]{4,3,2,1,0:T(8,128)S(1)} %get-tuple-element.29, f32[8,12,4,8]{3,2,1,0:T(4,128)S(1)} %get-tuple-element.28, pred[8,1024]{1,0:T(8,128)(4,1)S(1)} %broadcast_compare_fusion.1), kind=kLoop, calls=%fused_computation.12 | loop fusion | flops 15725568 | bytes 12615680 | tf_op jit(solution)/shard_map/reduce_sum | solution.py:29
  48.0 11.8 %all-to-all-start.2 = ((f32[32,3,4,8]{3,2,1,0:T(4,128)}), f32[32,3,4,8]{3,2,1,0:T(4,128)}, u32[]{:S(2)}, u32[]{:S(2)}) async-start(f32[32,3,4,8]{3,2,1,0:T(4,128)} %get-tuple-element.11), calls=%async_computation.2 | async-start | bytes 393216 | tf_op jit(solution)/shard_map/all_to_all | solution.py:178
  60.5 3.8 %convolution_bitcast_fusion.1 = f32[96,4,1,8,64]{4,3,1,0,2:T(8,128)} fusion(f32[96,4,1,8,32]{4,3,1,0,2:T(8,128)} %copy-done.4, bf16[96,32,1,128]{3,1,0,2:T(8,128)(2,1)} %bitcast.224, f32[96,4,8]{2,1,0:T(4,128)S(1)} %get-tuple-element.26, pred[96,32]{1,0:T(8,128)(4,1)} %broadcast_compare_fusion), kind=kOutput, calls=%fused_computation.30 | convolution fusion | flops 12877824 | bytes 1981440 | tf_op jit(solution)/shard_map/rtcju,rucd->rtcjd/dot_general | solution.py:137
  65.0 9.5 %fusion.16 = f32[8,12,4,1,8,64]{5,4,2,1,0,3:T(8,128)} fusion(bf16[8,1024,1,128]{3,1,2,0:T(8,128)(2,1)} %param.17, f32[8,12,4,8,1024]{4,3,2,1,0:T(8,128)} %copy-done.1, f32[8,12,4,8]{3,2,1,0:T(4,128)S(1)} %get-tuple-element.28, pred[8,1024]{1,0:T(8,128)(4,1)S(1)} %broadcast_compare_fusion.1), kind=kOutput, calls=%fused_computation.31 | convolution fusion | flops 418381824 | bytes 15679488 | tf_op jit(solution)/shard_map/grtcjp,gpcd->grtcjd/dot_general | solution.py:111
  81.1 3.2 gather_fusion.1
  92.9 3.2 multiply_add_fusion
  96.1 9.8 %all-to-all-start.1 = ((f32[32,3,4,8]{3,2,1,0:T(4,128)}), f32[32,3,4,8]{3,2,1,0:T(4,128)S(1)}, u32[]{:S(2)}, u32[]{:S(2)}) async-start(f32[32,3,4,8]{3,2,1,0:T(4,128)} %get-tuple-element.12), calls=%async_computation.1 | async-start | bytes 393216 | tf_op jit(solution)/shard_map/all_to_all | solution.py:177
  106.6 9.0 %all-to-all-done.1 = f32[32,3,4,8]{3,2,1,0:T(4,128)S(1)} async-done(((f32[32,3,4,8]{3,2,1,0:T(4,128)}), f32[32,3,4,8]{3,2,1,0:T(4,128)S(1)}, u32[]{:S(2)}, u32[]{:S(2)}) %all-to-all-start.1) | async-done | bytes 12320 | tf_op jit(solution)/shard_map/all_to_all | solution.py:177
  115.5 5.7 %all-to-all-start = ((f32[32,3,4,512]{3,2,1,0:T(4,128)}), f32[32,3,4,512]{3,2,1,0:T(4,128)}, u32[]{:S(2)}, u32[]{:S(2)}) async-start(f32[32,3,4,512]{3,2,1,0:T(4,128)} %multiply_add_fusion), calls=%async_computation | async-start | bytes 1572864 | tf_op jit(solution)/shard_map/all_to_all | solution.py:179
  129.8 2.7 reshape.444
  132.5 7.3 %all-to-all-done = f32[32,3,4,512]{3,2,1,0:T(4,128)} async-done(((f32[32,3,4,512]{3,2,1,0:T(4,128)}), f32[32,3,4,512]{3,2,1,0:T(4,128)}, u32[]{:S(2)}, u32[]{:S(2)}) %all-to-all-start) | async-done | bytes 786464 | tf_op jit(solution)/shard_map/all_to_all | solution.py:179
  143.1 63.7 %all-reduce.3.cloned.1.call-done = f32[12,2880]{1,0:T(8,128)} async-done(((f32[12,2880]{1,0:T(8,128)}), f32[12,2880]{1,0:T(8,128)}) %all-reduce.3.cloned.1.call-update) | async-done | bytes 138256 | tf_op jit(solution)/shard_map/psum | solution.py:195
  209.2 2.9 scatter_custom_fusion.1
  213.2 27.5 %all_to_all.25 = bf16[32,1,3,2880]{3,2,1,0:T(4,128)(2,1)S(1)} all-to-all(bf16[32,1,3,2880]{3,2,1,0:T(4,128)(2,1)} %bitcast.220), channel_id=1, replica_groups=mesh['seq'=32,'head'=8] {'seq'}, dimensions={0} | all-to-all | bytes 1105920 | tf_op jit(solution)/shard_map/all_to_all | solution.py:222
  240.7 3.7 %convolution_bitcast_fusion.2 = f32[32,1,3,720]{3,0,2,1:T(8,128)S(1)} fusion(bf16[2880,720,1]{0,1,2:T(8,128)(2,1)} %bitcast.217, bf16[32,1,3,2880]{3,2,1,0:T(4,128)(2,1)S(1)} %all_to_all.25), kind=kOutput, calls=%fused_computation.34 | convolution fusion | flops 398131200 | bytes 4976640 | tf_op jit(solution)/shard_map/nekd,edf->nekf/dot_general | solution.py:220
  247.2 7.7 %all-to-all-start.4 = ((f32[32,1,3,2880]{3,1,2,0:T(1,128)}), f32[32,1,3,2880]{3,1,2,0:T(1,128)}, u32[]{:S(2)}, u32[]{:S(2)}) async-start(f32[32,1,3,2880]{3,1,2,0:T(1,128)} %copy.142), calls=%async_computation.4 | async-start | bytes 2260992 | tf_op jit(solution)/shard_map/all_to_all | solution.py:231
  255.3 24.7 %all-to-all-done.4 = f32[32,1,3,2880]{3,1,2,0:T(1,128)} async-done(((f32[32,1,3,2880]{3,1,2,0:T(1,128)}), f32[32,1,3,2880]{3,1,2,0:T(1,128)}, u32[]{:S(2)}, u32[]{:S(2)}) %all-to-all-start.4) | async-done | bytes 1105952 | tf_op jit(solution)/shard_map/all_to_all | solution.py:231
  280.0 5.5 %reduce.6 = f32[32,3,2880]{2,1,0:T(4,128)} reduce(f32[32,1,3,2880]{3,1,2,0:T(1,128)} %all-to-all-done.4, f32[]{:T(128)} %constant.78), dimensions={1}, to_apply=%all_to_all.19.reduce_sub_computation | reduce | bytes 2211844 | tf_op jit(solution)/shard_map/all_to_all | solution.py:231
  288.1 3.0 gather_fusion.4
  293.5 66.7 %all-reduce.5.cloned.1.call-done = f32[12,2880]{1,0:T(8,128)} async-done(((f32[12,2880]{1,0:T(8,128)}), f32[12,2880]{1,0:T(8,128)}) %all-reduce.5.cloned.1.call-update) | async-done | bytes 138256 | tf_op jit(solution)/shard_map/psum | solution.py:243
  (140 shorter events, 66.7 us)
Async XLA Ops:
  6.5 134.9 %copy-start = (bf16[512,2880]{0,1:T(8,128)(2,1)S(1)}, bf16[512,2880]{0,1:T(8,128)(2,1)}, u32[]{:S(2)}) copy-start(bf16[512,2880]{0,1:T(8,128)(2,1)} %param.23) | copy-start | bytes 8847364
  6.5 16.0 %copy-start.24 = (f32[32]{0:T(128)}, f32[32]{0:T(128)S(1)}, u32[]{:S(2)}) copy-start(f32[32]{0:T(128)S(1)} %multiply_exponential_fusion) | copy-start | bytes 388
  11.6 29.2 %copy-start.19 = (s32[1024]{0:T(1024)}, s32[1024]{0:T(1024)S(1)}, u32[]{:S(2)}) copy-start(s32[1024]{0:T(1024)S(1)} %pad_clamp_fusion.2) | copy-start | bytes 12292
  14.4 8.2 %copy-start.9 = (f32[96,4]{1,0:T(8,128)}, f32[96,4]{1,0:T(8,128)S(1)}, u32[]{:S(2)}) copy-start(f32[96,4]{1,0:T(8,128)S(1)} %add_convert_fusion.2) | copy-start | bytes 4612
  35.5 4.6 %copy-start.1 = (f32[8,12,4,8,1024]{4,3,2,1,0:T(8,128)}, f32[8,12,4,8,1024]{4,3,2,1,0:T(8,128)S(1)}, u32[]{:S(2)}) copy-start(f32[8,12,4,8,1024]{4,3,2,1,0:T(8,128)S(1)} %get-tuple-element.29) | copy-start | bytes 37748740
  42.2 3.8 %copy-start.11 = (pred[96,32]{1,0:T(8,128)(4,1)S(1)}, pred[96,32]{1,0:T(8,128)(4,1)}, u32[]{:S(2)}) copy-start(pred[96,32]{1,0:T(8,128)(4,1)} %broadcast_compare_fusion) | copy-start | bytes 9220
  42.2 4.9 %copy-start.8 = (f32[96,4,8]{2,1,0:T(4,128)S(1)}, f32[96,4,8]{2,1,0:T(4,128)}, u32[]{:S(2)}) copy-start(f32[96,4,8]{2,1,0:T(4,128)} %gather_fusion.3) | copy-start | bytes 36868
  48.0 48.0 %all-to-all-start.2 = ((f32[32,3,4,8]{3,2,1,0:T(4,128)}), f32[32,3,4,8]{3,2,1,0:T(4,128)}, u32[]{:S(2)}, u32[]{:S(2)}) async-start(f32[32,3,4,8]{3,2,1,0:T(4,128)} %get-tuple-element.11), calls=%async_computation.2 | async-start | bytes 393216 | tf_op jit(solution)/shard_map/all_to_all | solution.py:178
  65.0 9.5 %copy-start.18 = (s32[96,4,4]{0,2,1:T(4,128)S(1)}, s32[96,4,4]{0,2,1:T(4,128)}, u32[]{:S(2)}) copy-start(s32[96,4,4]{0,2,1:T(4,128)} %param.26) | copy-start | bytes 18436
  74.5 3.6 copy-start.13
  74.5 3.6 copy-start.14
  92.9 28.6 %copy-start.25 = (f32[32]{0:T(128)S(1)}, f32[32]{0:T(128)}, u32[]{:S(2)}) copy-start(f32[32]{0:T(128)} %copy-done.24) | copy-start | bytes 388
  92.9 28.8 %copy-start.12 = (bf16[3,4,2880]{2,1,0:T(4,128)(2,1)S(1)}, bf16[3,4,2880]{2,1,0:T(4,128)(2,1)}, u32[]{:S(2)}) copy-start(bf16[3,4,2880]{2,1,0:T(4,128)(2,1)} %param.24) | copy-start | bytes 207364
  96.0 28.3 %copy-start.22 = (s32[48]{0:T(128)S(1)}, s32[48]{0:T(128)}, u32[]{:S(2)}) copy-start(s32[48]{0:T(128)} %copy-done.21) | copy-start | bytes 580
  96.1 19.5 %all-to-all-start.1 = ((f32[32,3,4,8]{3,2,1,0:T(4,128)}), f32[32,3,4,8]{3,2,1,0:T(4,128)S(1)}, u32[]{:S(2)}, u32[]{:S(2)}) async-start(f32[32,3,4,8]{3,2,1,0:T(4,128)} %get-tuple-element.12), calls=%async_computation.1 | async-start | bytes 393216 | tf_op jit(solution)/shard_map/all_to_all | solution.py:177
  115.5 24.3 %all-to-all-start = ((f32[32,3,4,512]{3,2,1,0:T(4,128)}), f32[32,3,4,512]{3,2,1,0:T(4,128)}, u32[]{:S(2)}, u32[]{:S(2)}) async-start(f32[32,3,4,512]{3,2,1,0:T(4,128)} %multiply_add_fusion), calls=%async_computation | async-start | bytes 1572864 | tf_op jit(solution)/shard_map/all_to_all | solution.py:179
  121.2 85.6 %all-reduce.3.cloned.1.call-start = ((), (), s32[]{:S(2)}) async-start(), calls=%async_computation.5 | async-start | bytes 376832 | tf_op jit(solution)/shard_map/psum | solution.py:195
  129.8 11.7 %copy-start.10 = (f32[12,512]{1,0:T(8,128)S(1)}, f32[12,512]{1,0:T(8,128)}, u32[]{:S(2)}) copy-start(f32[12,512]{1,0:T(8,128)} %reshape.448) | copy-start | bytes 73732
  141.4 67.1 %copy-start.16 = (f32[2880]{0:T(1024)S(1)}, f32[2880]{0:T(1024)}, u32[]{:S(2)}) copy-start(f32[2880]{0:T(1024)} %param.25) | copy-start | bytes 34564
  141.5 67.7 %copy-start.23 = (s32[48]{0:T(128)S(1)}, s32[48]{0:T(128)}, u32[]{:S(2)}) copy-start(s32[48]{0:T(128)} %fusion.82) | copy-start | bytes 580
  240.7 3.8 %copy-start.5 = (bf16[1,360,2880]{2,1,0:T(8,128)(2,1)S(1)}, bf16[1,360,2880]{2,1,0:T(8,128)(2,1)}, u32[]{:S(2)}) copy-start(bf16[1,360,2880]{2,1,0:T(8,128)(2,1)} %param.29) | copy-start | bytes 6220804
  245.0 10.2 %copy-start.20 = (f32[3,4,4]{2,1,0:T(4,128)S(1)}, f32[3,4,4]{2,1,0:T(4,128)}, u32[]{:S(2)}) copy-start(f32[3,4,4]{2,1,0:T(4,128)} %param.27) | copy-start | bytes 580
  247.2 32.8 %all-to-all-start.4 = ((f32[32,1,3,2880]{3,1,2,0:T(1,128)}), f32[32,1,3,2880]{3,1,2,0:T(1,128)}, u32[]{:S(2)}, u32[]{:S(2)}) async-start(f32[32,1,3,2880]{3,1,2,0:T(1,128)} %copy.142), calls=%async_computation.4 | async-start | bytes 2260992 | tf_op jit(solution)/shard_map/all_to_all | solution.py:231
  254.9 105.2 %all-reduce.5.cloned.1.call-start = ((), (), s32[]{:S(2)}) async-start(), calls=%async_computation.6 | async-start | bytes 376832 | tf_op jit(solution)/shard_map/psum | solution.py:243
  (9 other events, 16.1 us)
Sparse Core Ops, SparseCore 0:
  143.2 63.5 all-reduce.2
  293.6 66.4 all-reduce.4
where the time goes:
time: 370 us; the launch traced here: 369 us
  waiting for transfers between devices  171 us (46%)
  local copies, waits for them, and re-layouts  57 us (15%)
  other arithmetic  36.6 us (10%)
  starting transfers between devices  35.5 us (10%)
  blocking collectives  27.5 us (7%)
  matrix products  26.8 us (7%)
  between operations  13.9 us (4%)
    psum x1, waiting for transfers between devices, on_device(): expert_total = lax.psum(expert_part, 'head')  66.7 us
    psum x1, waiting for transfers between devices, on_device(): projected = lax.psum(partial_proj, 'head')  63.7 us
    all_to_all x1, blocking collectives, on_device(): lax.all_to_all(outgoing, 'seq', split_axis=0, concat_axis=0, tiled=True)  27.5 us
    all_to_all x1, waiting for transfers between devices, on_device(): lax.all_to_all(jnp.einsum('nekf,efd->nekd', activation, down_weight, pref...  24.7 us
    all_to_all x1, starting transfers between devices, on_device(): lax.all_to_all(by_owner[1], 'seq', split_axis=0, concat_axis=0, tiled=True)  11.8 us
    unnamed x58, local copies, waits for them, and re-layouts  11.2 us
    all_to_all x1, starting transfers between devices, on_device(): lax.all_to_all(by_owner[0], 'seq', split_axis=0, concat_axis=0, tiled=True)  9.79 us
    dot_general x1, matrix products, on_device(): jnp.einsum('grtcjp,gpcd->grtcjd', prompt_weights.astype(jnp.bfloat16), pr...  9.51 us
  transfers between devices with their start and end apart: 6, of which 5 were waited for; matrix products, arithmetic and copies ran while one was open for 13% of the time, Pallas kernels for 0%

commit v1 on v0

--- a/solution.py
+++ b/solution.py
@@ -192,7 +192,8 @@
     partial_proj = jnp.dot(
         attended.reshape(token_count, query_width), o_weight, preferred_element_type=jnp.float32
     )
-    projected = lax.psum(partial_proj, "head")
+    arr_next = lax.all_gather(partial_proj, "head")
+    projected = jnp.sum(arr_next, axis=0)
     hidden = (resid.reshape(token_count, model_width).astype(jnp.float32) + projected).astype(
         jnp.bfloat16
     )

time: 370 us -> 330 us (0.89)
  waiting for transfers between devices: 171 us -> 131 us
    psum x1 -> x0, waiting for transfers between devices: 63.7 us -> none  [on_device(): projected = lax.psum(partial_proj, 'head')]
    all_gather x0 -> x1, waiting for transfers between devices: none -> 24.6 us  [on_device(): arr_next = lax.all_gather(partial_proj, 'head')]
    psum x1, waiting for transfers between devices: 66.7 us -> 62.5 us  [on_device(): expert_total = lax.psum(expert_part, 'head')]
    unnamed x58 -> x38, local copies, waits for them, and re-layouts: 11.2 us -> 10.1 us
where the time goes in v1:
time: 330 us; the launch traced here: 328 us
  waiting for transfers between devices  131 us (40%)
  local copies, waits for them, and re-layouts  54.8 us (17%)
  other arithmetic  35.9 us (11%)
  starting transfers between devices  35.3 us (11%)
  blocking collectives  30.5 us (9%)
  matrix products  26.8 us (8%)
  between operations  13.8 us (4%)
    psum x1, waiting for transfers between devices, on_device(): expert_total = lax.psum(expert_part, 'head')  62.5 us
    all_to_all x1, blocking collectives, on_device(): lax.all_to_all(outgoing, 'seq', split_axis=0, concat_axis=0, tiled=True)  30.5 us
    all_to_all x1, waiting for transfers between devices, on_device(): lax.all_to_all(jnp.einsum('nekf,efd->nekd', activation, down_weight, pref...  27.2 us
    all_gather x1, waiting for transfers between devices, on_device(): arr_next = lax.all_gather(partial_proj, 'head')  24.6 us
    all_to_all x1, starting transfers between devices, on_device(): lax.all_to_all(by_owner[1], 'seq', split_axis=0, concat_axis=0, tiled=True)  11.8 us
    unnamed x38, local copies, waits for them, and re-layouts  10.1 us
    all_to_all x1, waiting for transfers between devices, on_device(): lax.all_to_all(by_owner[2], 'seq', split_axis=0, concat_axis=0, tiled=True)  9.98 us
    all_to_all x1, starting transfers between devices, on_device(): lax.all_to_all(by_owner[0], 'seq', split_axis=0, concat_axis=0, tiled=True)  9.78 us
  transfers between devices with their start and end apart: 6, of which 5 were waited for; matrix products, arithmetic and copies ran while one was open for 13% of the time, Pallas kernels for 0%

profile of v1, /device:TPU:8, one launch (start us, length us, event | category | flops | bytes accessed | tf_op | source)
XLA Modules:
  0.0 328.1 jit_solution(16924144192745075541)
XLA Ops:
  7.5 3.2 sort.17
  16.9 3.4 %copy.153 = f32[96,4,8,32]{3,2,1,0:T(8,128)} copy(f32[96,4,8,32]{0,3,2,1:T(8,128)} %get-tuple-element.15) | data formatting | bytes 786432
  29.1 2.7 gather_fusion
  31.8 3.7 %fusion.1 = (f32[8,12,4,8]{3,2,1,0:T(4,128)S(1)}, f32[8,12,4,8,1024]{4,3,2,1,0:T(8,128)S(1)}) fusion(pred[8,1024]{1,0:T(8,128)(4,1)S(1)} %broadcast_compare_fusion.1, bf16[8,12,4,8,64]{4,3,2,1,0:T(8,128)(2,1)} %bitcast.217, bf16[8,1024,1,128]{3,1,2,0:T(8,128)(2,1)} %param.17), kind=kOutput, calls=%fused_computation.11 | convolution fusion | flops 412087296 | bytes 15093760 | tf_op jit(solution)/shard_map/grtcjd,gpcd->grtcjp/dot_general | solution.py:97
  35.5 4.0 %fusion.2 = f32[8,12,4,8]{3,2,1,0:T(4,128)S(1)} fusion(f32[8,12,4,8,1024]{4,3,2,1,0:T(8,128)S(1)} %get-tuple-element.29, f32[8,12,4,8]{3,2,1,0:T(4,128)S(1)} %get-tuple-element.28, pred[8,1024]{1,0:T(8,128)(4,1)S(1)} %broadcast_compare_fusion.1), kind=kLoop, calls=%fused_computation.12 | loop fusion | flops 15725568 | bytes 12615680 | tf_op jit(solution)/shard_map/reduce_sum | solution.py:29
  48.0 11.8 %all-to-all-start.2 = ((f32[32,3,4,8]{3,2,1,0:T(4,128)}), f32[32,3,4,8]{3,2,1,0:T(4,128)}, u32[]{:S(2)}, u32[]{:S(2)}) async-start(f32[32,3,4,8]{3,2,1,0:T(4,128)} %get-tuple-element.11), calls=%async_computation.2 | async-start | bytes 393216 | tf_op jit(solution)/shard_map/all_to_all | solution.py:178
  60.5 3.7 %convolution_bitcast_fusion.2 = f32[96,4,1,8,64]{4,3,1,0,2:T(8,128)} fusion(f32[96,4,1,8,32]{4,3,1,0,2:T(8,128)} %copy-done.4, bf16[96,32,1,128]{3,1,0,2:T(8,128)(2,1)} %bitcast.226, f32[96,4,8]{2,1,0:T(4,128)S(1)} %get-tuple-element.26, pred[96,32]{1,0:T(8,128)(4,1)} %broadcast_compare_fusion), kind=kOutput, calls=%fused_computation.31 | convolution fusion | flops 12877824 | bytes 1981440 | tf_op jit(solution)/shard_map/rtcju,rucd->rtcjd/dot_general | solution.py:137
  64.3 9.6 %fusion.16 = f32[8,12,4,1,8,64]{5,4,2,1,0,3:T(8,128)} fusion(bf16[8,1024,1,128]{3,1,2,0:T(8,128)(2,1)} %param.17, f32[8,12,4,8,1024]{4,3,2,1,0:T(8,128)} %copy-done.1, f32[8,12,4,8]{3,2,1,0:T(4,128)S(1)} %get-tuple-element.28, pred[8,1024]{1,0:T(8,128)(4,1)S(1)} %broadcast_compare_fusion.1), kind=kOutput, calls=%fused_computation.32 | convolution fusion | flops 418381824 | bytes 15679488 | tf_op jit(solution)/shard_map/grtcjp,gpcd->grtcjd/dot_general | solution.py:111
  73.9 2.7 reshape.451
  79.6 3.0 gather_fusion.1
  91.2 9.8 %all-to-all-start.1 = ((f32[32,3,4,8]{3,2,1,0:T(4,128)}), f32[32,3,4,8]{3,2,1,0:T(4,128)S(1)}, u32[]{:S(2)}, u32[]{:S(2)}) async-start(f32[32,3,4,8]{3,2,1,0:T(4,128)} %get-tuple-element.12), calls=%async_computation.1 | async-start | bytes 393216 | tf_op jit(solution)/shard_map/all_to_all | solution.py:177
  101.0 3.1 multiply_add_fusion
  104.2 6.5 %all-to-all-done.1 = f32[32,3,4,8]{3,2,1,0:T(4,128)S(1)} async-done(((f32[32,3,4,8]{3,2,1,0:T(4,128)}), f32[32,3,4,8]{3,2,1,0:T(4,128)S(1)}, u32[]{:S(2)}, u32[]{:S(2)}) %all-to-all-start.1) | async-done | bytes 12320 | tf_op jit(solution)/shard_map/all_to_all | solution.py:177
  110.7 5.7 %all-to-all-start = ((f32[32,3,4,512]{3,2,1,0:T(4,128)}), f32[32,3,4,512]{3,2,1,0:T(4,128)}, u32[]{:S(2)}, u32[]{:S(2)}) async-start(f32[32,3,4,512]{3,2,1,0:T(4,128)} %multiply_add_fusion), calls=%async_computation | async-start | bytes 1572864 | tf_op jit(solution)/shard_map/all_to_all | solution.py:179
  125.0 10.0 %all-to-all-done = f32[32,3,4,512]{3,2,1,0:T(4,128)} async-done(((f32[32,3,4,512]{3,2,1,0:T(4,128)}), f32[32,3,4,512]{3,2,1,0:T(4,128)}, u32[]{:S(2)}, u32[]{:S(2)}) %all-to-all-start) | async-done | bytes 786464 | tf_op jit(solution)/shard_map/all_to_all | solution.py:179
  139.4 24.6 %all-gather.4.cloned.1.call-done = f32[8,12,2880]{2,1,0:T(8,128)} async-done(((f32[1,12,2880]{2,1,0:T(8,128)}), f32[8,12,2880]{2,1,0:T(8,128)}) %all-gather.4.cloned.1.call-update) | async-done | bytes 1105936 | tf_op jit(solution)/shard_map/all_gather | solution.py:195
  167.3 3.0 scatter_custom_fusion.1
  171.4 30.5 %all_to_all.25 = bf16[32,1,3,2880]{3,2,1,0:T(4,128)(2,1)S(1)} all-to-all(bf16[32,1,3,2880]{3,2,1,0:T(4,128)(2,1)} %bitcast.222), channel_id=1, replica_groups=mesh['seq'=32,'head'=8] {'seq'}, dimensions={0} | all-to-all | bytes 1105920 | tf_op jit(solution)/shard_map/all_to_all | solution.py:223
  201.9 3.7 %convolution_bitcast_fusion.3 = f32[32,1,3,720]{3,0,2,1:T(8,128)S(1)} fusion(bf16[2880,720,1]{0,1,2:T(8,128)(2,1)} %bitcast.219, bf16[32,1,3,2880]{3,2,1,0:T(4,128)(2,1)S(1)} %all_to_all.25), kind=kOutput, calls=%fused_computation.35 | convolution fusion | flops 398131200 | bytes 4976640 | tf_op jit(solution)/shard_map/nekd,edf->nekf/dot_general | solution.py:221
  208.4 7.5 %all-to-all-start.4 = ((f32[32,1,3,2880]{3,1,2,0:T(1,128)}), f32[32,1,3,2880]{3,1,2,0:T(1,128)}, u32[]{:S(2)}, u32[]{:S(2)}) async-start(f32[32,1,3,2880]{3,1,2,0:T(1,128)} %copy.142), calls=%async_computation.4 | async-start | bytes 2260992 | tf_op jit(solution)/shard_map/all_to_all | solution.py:232
  216.3 27.2 %all-to-all-done.4 = f32[32,1,3,2880]{3,1,2,0:T(1,128)} async-done(((f32[32,1,3,2880]{3,1,2,0:T(1,128)}), f32[32,1,3,2880]{3,1,2,0:T(1,128)}, u32[]{:S(2)}, u32[]{:S(2)}) %all-to-all-start.4) | async-done | bytes 1105952 | tf_op jit(solution)/shard_map/all_to_all | solution.py:232
  243.5 5.5 %reduce.8 = f32[32,3,2880]{2,1,0:T(4,128)} reduce(f32[32,1,3,2880]{3,1,2,0:T(1,128)} %all-to-all-done.4, f32[]{:T(128)} %constant.78), dimensions={1}, to_apply=%all_to_all.19.reduce_sub_computation | reduce | bytes 2211844 | tf_op jit(solution)/shard_map/all_to_all | solution.py:232
  251.7 3.0 gather_fusion.4
  257.1 62.5 %all-reduce.2.cloned.1.call-done = f32[12,2880]{1,0:T(8,128)} async-done(((f32[12,2880]{1,0:T(8,128)}), f32[12,2880]{1,0:T(8,128)}) %all-reduce.2.cloned.1.call-update) | async-done | bytes 138256 | tf_op jit(solution)/shard_map/psum | solution.py:244
  (123 shorter events, 63.8 us)
Async XLA Ops:
  6.5 130.1 %copy-start = (bf16[512,2880]{0,1:T(8,128)(2,1)S(1)}, bf16[512,2880]{0,1:T(8,128)(2,1)}, u32[]{:S(2)}) copy-start(bf16[512,2880]{0,1:T(8,128)(2,1)} %param.23) | copy-start | bytes 8847364
  14.4 8.2 %copy-start.9 = (f32[96,4]{1,0:T(8,128)}, f32[96,4]{1,0:T(8,128)S(1)}, u32[]{:S(2)}) copy-start(f32[96,4]{1,0:T(8,128)S(1)} %add_convert_fusion.3) | copy-start | bytes 4612
  16.9 3.4 %copy-start.6 = (f32[96,4,8,32]{0,3,2,1:T(8,128)S(1)}, f32[96,4,8,32]{0,3,2,1:T(8,128)}, u32[]{:S(2)}) copy-start(f32[96,4,8,32]{0,3,2,1:T(8,128)} %get-tuple-element.16) | copy-start | bytes 1179652
  26.6 0.9 copy-start.2
  26.6 1.1 copy-start.3
  35.5 4.6 %copy-start.1 = (f32[8,12,4,8,1024]{4,3,2,1,0:T(8,128)}, f32[8,12,4,8,1024]{4,3,2,1,0:T(8,128)S(1)}, u32[]{:S(2)}) copy-start(f32[8,12,4,8,1024]{4,3,2,1,0:T(8,128)S(1)} %get-tuple-element.29) | copy-start | bytes 37748740
  42.2 3.8 %copy-start.10 = (pred[96,32]{1,0:T(8,128)(4,1)S(1)}, pred[96,32]{1,0:T(8,128)(4,1)}, u32[]{:S(2)}) copy-start(pred[96,32]{1,0:T(8,128)(4,1)} %broadcast_compare_fusion) | copy-start | bytes 9220
  42.2 5.0 %copy-start.7 = (f32[96,4,8]{2,1,0:T(4,128)S(1)}, f32[96,4,8]{2,1,0:T(4,128)}, u32[]{:S(2)}) copy-start(f32[96,4,8]{2,1,0:T(4,128)} %gather_fusion.3) | copy-start | bytes 36868
  44.8 1.2 copy-start.4
  48.0 43.2 %all-to-all-start.2 = ((f32[32,3,4,8]{3,2,1,0:T(4,128)}), f32[32,3,4,8]{3,2,1,0:T(4,128)}, u32[]{:S(2)}, u32[]{:S(2)}) async-start(f32[32,3,4,8]{3,2,1,0:T(4,128)} %get-tuple-element.11), calls=%async_computation.2 | async-start | bytes 393216 | tf_op jit(solution)/shard_map/all_to_all | solution.py:178
  64.3 9.6 %copy-start.11 = (f32[96,4,8]{0,2,1:T(8,128)S(1)}, f32[96,4,8]{0,2,1:T(8,128)}, u32[]{:S(2)}) copy-start(f32[96,4,8]{0,2,1:T(8,128)} %copy.131) | copy-start | bytes 36868
  91.2 19.5 %all-to-all-start.1 = ((f32[32,3,4,8]{3,2,1,0:T(4,128)}), f32[32,3,4,8]{3,2,1,0:T(4,128)S(1)}, u32[]{:S(2)}, u32[]{:S(2)}) async-start(f32[32,3,4,8]{3,2,1,0:T(4,128)} %get-tuple-element.12), calls=%async_computation.1 | async-start | bytes 393216 | tf_op jit(solution)/shard_map/all_to_all | solution.py:177
  101.0 16.4 %copy-start.12 = (bf16[3,4,1,128]{3,1,2,0:T(4,128)(2,1)S(1)}, bf16[3,4,1,128]{3,1,2,0:T(4,128)(2,1)}, u32[]{:S(2)}) copy-start(bf16[3,4,1,128]{3,1,2,0:T(4,128)(2,1)} %param.16) | copy-start | bytes 9220
  104.2 16.0 %copy-start.16 = (f32[8]{0:T(128)S(1)}, f32[8]{0:T(128)}, u32[]{:S(2)}) copy-start(f32[8]{0:T(128)} %param.19) | copy-start | bytes 100
  110.7 24.3 %all-to-all-start = ((f32[32,3,4,512]{3,2,1,0:T(4,128)}), f32[32,3,4,512]{3,2,1,0:T(4,128)}, u32[]{:S(2)}, u32[]{:S(2)}) async-start(f32[32,3,4,512]{3,2,1,0:T(4,128)} %multiply_add_fusion), calls=%async_computation | async-start | bytes 1572864 | tf_op jit(solution)/shard_map/all_to_all | solution.py:179
  116.4 47.7 %all-gather.4.cloned.1.call-start = ((), (), s32[]{:S(2)}) async-start(), calls=%async_computation.6 | async-start | bytes 1695744 | tf_op jit(solution)/shard_map/all_gather | solution.py:195
  136.6 1.6 copy-start.8
  136.6 1.7 copy-start.13
  201.9 3.8 %copy-start.5 = (bf16[1,360,2880]{2,1,0:T(8,128)(2,1)S(1)}, bf16[1,360,2880]{2,1,0:T(8,128)(2,1)}, u32[]{:S(2)}) copy-start(bf16[1,360,2880]{2,1,0:T(8,128)(2,1)} %param.29) | copy-start | bytes 6220804
  206.2 10.0 %copy-start.14 = (f32[3,4,4]{2,1,0:T(4,128)S(1)}, f32[3,4,4]{2,1,0:T(4,128)}, u32[]{:S(2)}) copy-start(f32[3,4,4]{2,1,0:T(4,128)} %param.27) | copy-start | bytes 580
  206.2 10.0 %copy-start.15 = (s32[48]{0:T(128)S(1)}, s32[48]{0:T(128)}, u32[]{:S(2)}) copy-start(s32[48]{0:T(128)} %fusion.80) | copy-start | bytes 580
  208.4 35.1 %all-to-all-start.4 = ((f32[32,1,3,2880]{3,1,2,0:T(1,128)}), f32[32,1,3,2880]{3,1,2,0:T(1,128)}, u32[]{:S(2)}, u32[]{:S(2)}) async-start(f32[32,1,3,2880]{3,1,2,0:T(1,128)} %copy.142), calls=%async_computation.4 | async-start | bytes 2260992 | tf_op jit(solution)/shard_map/all_to_all | solution.py:232
  215.9 103.6 %all-reduce.2.cloned.1.call-start = ((), (), s32[]{:S(2)}) async-start(), calls=%async_computation.5 | async-start | bytes 376832 | tf_op jit(solution)/shard_map/psum | solution.py:244
Sparse Core Ops, SparseCore 0:
  138.3 25.7 all-gather.3
  257.2 62.3 all-reduce.1
